TPU v7x, 512 devices: a whole 4x4x16 slice. The times are simulated.
512 devices in a mesh: wide: 64 (over y, z_lo, core), narrow: 8 (over x, z_hi).
Axes of the slice: x: 4, y: 4, z: 16 (z_hi: 2, z_lo: 8; z = z_hi * 8 + z_lo), core: 2. Of those that a mesh axis runs over, the one named last changes fastest.
Arguments:
- tensor: bfloat16 [16, 4096, 8192], P('narrow', 'wide'), may hold values from -16 to 16
- factor_a: bfloat16 [32, 4096], P(None, 'wide'), may hold values from -0.21875 to 0.21875
- factor_b: bfloat16 [32, 8192], P(None, 'wide'), may hold values from -0.15625 to 0.15625
- factor_c: bfloat16 [32, 16], P(None, 'narrow'), may hold values from -4 to 4
Outputs:
- step_a: float32 [32, 4096], P(None, 'wide')
- step_b: float32 [32, 8192], P(None, 'wide')
- step_c: float32 [32, 16], P(None, 'narrow')
All inputs are finite; a program needn't handle non-finite values.
Results may differ from a plain program's by a relative error of at most 0.0029.
Values may be sent and summed in bfloat16 or wider, within the bound.
No kernel may reach another device: no remote copies, remote signals or barrier semaphores. Data moves between devices by JAX's collectives and lax.ppermute only.
A program may use at most 64 MiB of HBM per device.

v0:
```python
import jax
import jax.numpy as jnp
from jax import lax
from jax.sharding import PartitionSpec as P

ITERS = 2
damping = 1.0
highest = lax.Precision.HIGHEST


def matmul(left, right):
    return jnp.dot(left, right, precision=highest)


def outer_rows(left, right):
    return lax.dot_general(left, right, (((1,), (1,)), ((), ())), precision=highest)


def combine_dot(wide_part, narrow_part):
    return lax.psum(wide_part, "wide") + lax.psum(narrow_part, "narrow")


def self_inner(triple):
    return combine_dot(
        jnp.sum(triple[0] * triple[0]) + jnp.sum(triple[1] * triple[1]),
        jnp.sum(triple[2] * triple[2]),
    )


def gram_product(factors, grams, directions):
    float_a, float_b, float_c = factors
    gram_a, gram_b, gram_c = grams
    dir_a, dir_b, dir_c = directions
    local_a = outer_rows(float_a, dir_a)
    local_b = outer_rows(float_b, dir_b)
    local_c = outer_rows(float_c, dir_c)
    cross_a, cross_b = lax.psum((local_a, local_b), "wide")
    cross_c = lax.psum(local_c, "narrow")
    hadamard_a = gram_b * gram_c
    hadamard_b = gram_a * gram_c
    hadamard_c = gram_a * gram_b
    mixed_a = cross_b * gram_c + gram_b * cross_c
    mixed_b = cross_a * gram_c + gram_a * cross_c
    mixed_c = cross_a * gram_b + gram_a * cross_b
    image_a = matmul(hadamard_a, dir_a) + matmul(mixed_a, float_a) + damping * dir_a
    image_b = matmul(hadamard_b, dir_b) + matmul(mixed_b, float_b) + damping * dir_b
    image_c = matmul(hadamard_c, dir_c) + matmul(mixed_c, float_c) + damping * dir_c
    curvature = combine_dot(
        jnp.sum(dir_a * image_a) + jnp.sum(dir_b * image_b), jnp.sum(dir_c * image_c)
    )
    return ((image_a, image_b, image_c), curvature)


def on_device(tensor, factor_a, factor_b, factor_c):
    k_local, i_local, j_whole = tensor.shape
    rank = factor_a.shape[0]
    j_local = factor_b.shape[1]
    flattened = tensor.reshape(k_local * i_local, j_whole)
    contracted = lax.dot_general(
        lax.all_gather(factor_b, "wide", axis=1, tiled=True),
        flattened,
        (((1,), (1,)), ((), ())),
        preferred_element_type=jnp.float32,
    ).reshape(rank, k_local, i_local)
    float_a = factor_a.astype(jnp.float32)
    float_b = factor_b.astype(jnp.float32)
    float_c = factor_c.astype(jnp.float32)
    part_a = jnp.einsum("rk,rki->ri", float_c, contracted, precision=highest)
    part_c = jnp.einsum("ri,rki->rk", float_a, contracted, precision=highest)
    own_gram_a = jnp.dot(factor_a, factor_a.T, preferred_element_type=jnp.float32)
    own_gram_b = jnp.dot(factor_b, factor_b.T, preferred_element_type=jnp.float32)
    own_gram_c = jnp.dot(factor_c, factor_c.T, preferred_element_type=jnp.float32)
    mttkrp_a, gram_c = lax.psum((part_a, own_gram_c), "narrow")
    mttkrp_c, gram_a, gram_b = lax.psum((part_c, own_gram_a, own_gram_b), "wide")
    khatri = (
        (float_c[:, :, None] * float_a[:, None, :])
        .reshape(rank, k_local * i_local)
        .astype(jnp.bfloat16)
    )
    partial_b = jnp.dot(khatri, flattened, preferred_element_type=jnp.float32)
    total_b = lax.psum(partial_b, ("wide", "narrow"))
    mttkrp_b = lax.dynamic_slice_in_dim(total_b, lax.axis_index("wide") * j_local, j_local, 1)
    grad_a = matmul(gram_b * gram_c, float_a) - mttkrp_a
    grad_b = matmul(gram_a * gram_c, float_b) - mttkrp_b
    grad_c = matmul(gram_a * gram_b, float_c) - mttkrp_c
    factors = (float_a, float_b, float_c)
    grams = (gram_a, gram_b, gram_c)
    resid = (-grad_a, -grad_b, -grad_c)
    direction = resid
    steps = (jnp.zeros_like(grad_a), jnp.zeros_like(grad_b), jnp.zeros_like(grad_c))
    norm_now = self_inner(resid)
    for iteration in range(ITERS):
        image, curvature = gram_product(factors, grams, direction)
        step_size = norm_now / curvature
        steps = tuple((old + step_size * move for old, move in zip(steps, direction)))
        if iteration + 1 < ITERS:
            resid = tuple((old - step_size * move for old, move in zip(resid, image)))
            norm_next = self_inner(resid)
            momentum = norm_next / norm_now
            direction = tuple((now + momentum * old for now, old in zip(resid, direction)))
            norm_now = norm_next
    return (steps[0], steps[1], steps[2])


def solution(mesh):
    placed = (P("narrow", "wide", None), P(None, "wide"), P(None, "wide"), P(None, "narrow"))
    return jax.shard_map(
        on_device,
        mesh=mesh,
        in_specs=placed,
        out_specs=(P(None, "wide"), P(None, "wide"), P(None, "narrow")),
        check_vma=False,
    )
```

profile of v0, /device:TPU:1, one launch (start us, length us, event | category | flops | bytes accessed | tf_op | source)
XLA Modules:
  0.0 2312.1 jit_solution(18251631645562315056)
XLA Ops:
  7.2 0.8 convert_element_type.12
  8.1 0.7 convert_element_type.11
  8.8 1.6 convolution_bitcast_fusion
  10.4 0.2 fusion.51
  10.6 129.4 %all_gather.3 = bf16[32,8192]{1,0:T(8,128)(2,1)S(1)} all-gather(bf16[32,128]{1,0:T(8,128)(2,1)S(1)} %copy-done.1), channel_id=1, replica_groups=mesh['wide'=64,'narrow'=8] {'wide'}, dimensions={1}, use_global_device_ids=true | all-gather | bytes 532480 | tf_op jit(solution)/shard_map/all_gather | solution.py:60
  140.0 0.1 fusion.50
  140.1 0.1 fusion.52
  140.2 0.1 copy.14
  140.3 1.1 fusion.12
  141.4 0.3 fusion.16
  141.7 0.2 fusion.14
  141.9 66.7 %all-reduce.6 = (f32[32,32]{1,0:T(8,128)S(1)}, f32[32,64]{1,0:T(8,128)S(1)}) all-reduce(f32[32,32]{1,0:T(8,128)S(1)} %fusion.51, f32[32,64]{1,0:T(8,128)S(1)} %bitcast.63), channel_id=1, replica_groups=mesh['wide'=64,'narrow'=8] {'narrow'}, use_global_device_ids=true, to_apply=%region_1.0 | all-reduce | flops 3072 | bytes 24576 | tf_op jit(solution)/shard_map/psum | solution.py:73
  208.7 415.4 %all-reduce.3 = (f32[32,32]{1,0:T(8,128)S(1)}, f32[32,32]{1,0:T(8,128)S(1)}) all-reduce(f32[32,32]{1,0:T(8,128)S(1)} %fusion.50, f32[32,32]{1,0:T(8,128)S(1)} %fusion.52), channel_id=1, replica_groups=mesh['wide'=64,'narrow'=8] {'wide'}, use_global_device_ids=true, to_apply=%region_0.0 | all-reduce | flops 2048 | bytes 16384 | tf_op jit(solution)/shard_map/psum | solution.py:74
  624.1 0.1 convolution_subtract_fusion.1
  624.3 0.1 convolution_bitcast_fusion.4
  624.4 0.2 fusion.45
  624.6 0.8 convolution_subtract_fusion
  625.4 0.1 convolution_bitcast_fusion.6
  625.6 0.2 fusion.41
  625.7 418.8 %all-reduce.2 = (f32[32,2]{0,1:T(2,128)S(1)}, f32[32,32]{1,0:T(8,128)S(1)}, f32[32,32]{1,0:T(8,128)S(1)}) all-reduce(f32[32,2]{0,1:T(2,128)S(1)} %bitcast.64, f32[32,32]{1,0:T(8,128)S(1)} %convolution_bitcast_fusion.6, f32[32,32]{1,0:T(8,128)S(1)} %convolution_bitcast_fusion.4), channel_id=1, replica_groups=mesh['wide'=64,'narrow'=8] {'wide'}, use_global_device_ids=true, to_apply=%region_8.0 | all-reduce | flops 2112 | bytes 16896 | tf_op jit(solution)/shard_map/psum | solution.py:74
  1044.5 0.1 convolution_subtract_fusion.2
  1044.6 0.2 convolution_bitcast_fusion.5
  1044.8 0.1 fusion.28
  1045.0 0.8 multiply_reduce_fusion.7
  1045.7 60.0 %all-reduce.5 = (f32[32,32]{1,0:T(8,128)S(1)}, f32[]{:T(128)}, f32[]{:T(128)}) all-reduce(f32[32,32]{1,0:T(8,128)S(1)} %convolution_bitcast_fusion.5, f32[]{:T(128)} %get-tuple-element.8, f32[]{:T(128)} %get-tuple-element.7), channel_id=1, replica_groups=mesh['wide'=64,'narrow'=8] {'narrow'}, use_global_device_ids=true, to_apply=%region_12.0 | all-reduce | flops 1026 | bytes 8208 | tf_op jit(solution)/shard_map/psum | solution.py:38
  1105.8 0.8 multiply_reduce_fusion.3
  1106.6 0.8 multiply_reduce_fusion.2
  1109.9 228.5 %all-reduce.1 = (f32[]{:T(128)}, f32[]{:T(128)}) all-reduce(f32[]{:T(128)S(6)} %add.140, f32[]{:T(128)S(6)} %add.148), channel_id=1, replica_groups=mesh['wide'=64,'narrow'=8] {'wide'}, use_global_device_ids=true, to_apply=%region_7.0 | all-reduce | flops 2 | bytes 16 | tf_op jit(solution)/shard_map/psum | solution.py:20
  1341.1 0.6 multiply_reduce_fusion.1
  1341.7 0.6 multiply_reduce_fusion
  1343.6 0.6 multiply_reduce_fusion.6
  1344.2 210.8 %psum.153 = f32[]{:T(128)} all-reduce(f32[]{:T(128)S(6)} %add.153), channel_id=1, replica_groups=mesh['wide'=64,'narrow'=8] {'wide'}, use_global_device_ids=true, to_apply=%region_21.0 | all-reduce | flops 1 | bytes 8 | tf_op jit(solution)/shard_map/psum | solution.py:20
  1555.0 38.4 %psum.154 = f32[]{:T(128)} all-reduce(f32[]{:T(128)} %multiply_reduce_fusion.6), channel_id=1, replica_groups=mesh['wide'=64,'narrow'=8] {'narrow'}, use_global_device_ids=true, to_apply=%region_23.0 | all-reduce | flops 1 | bytes 8 | tf_op jit(solution)/shard_map/psum | solution.py:20
  1594.8 0.1 fusion.53
  1594.9 0.1 convolution_bitcast_fusion.1
  1595.1 0.1 convolution_bitcast_fusion.3
  1595.2 0.2 fusion.54
  1595.4 0.2 convolution_bitcast_fusion.2
  1595.6 412.3 %all-reduce = (f32[32,32]{1,0:T(8,128)S(1)}, f32[32,32]{1,0:T(8,128)S(1)}) all-reduce(f32[32,32]{1,0:T(8,128)S(1)} %convolution_bitcast_fusion.3, f32[32,32]{1,0:T(8,128)S(1)} %convolution_bitcast_fusion.1), channel_id=1, replica_groups=mesh['wide'=64,'narrow'=8] {'wide'}, use_global_device_ids=true, to_apply=%region_24.0 | all-reduce | flops 2048 | bytes 16384 | tf_op jit(solution)/shard_map/psum | solution.py:37
  2007.9 0.1 fusion.18
  2008.0 0.8 fusion.11
  2008.8 62.2 %all-reduce.4 = (f32[32,32]{1,0:T(8,128)S(1)}, f32[]{:T(128)}) all-reduce(f32[32,32]{1,0:T(8,128)S(1)} %convolution_bitcast_fusion.2, f32[]{:T(128)} %fusion.11), channel_id=1, replica_groups=mesh['wide'=64,'narrow'=8] {'narrow'}, use_global_device_ids=true, to_apply=%region_25.0 | all-reduce | flops 1025 | bytes 8200 | tf_op jit(solution)/shard_map/psum | solution.py:38
  2071.0 0.7 fusion.9
  2071.7 0.7 fusion.10
  2073.7 228.4 %psum.158 = f32[]{:T(128)} all-reduce(f32[]{:T(128)S(6)} %add.164), channel_id=1, replica_groups=mesh['wide'=64,'narrow'=8] {'wide'}, use_global_device_ids=true, to_apply=%region_29.0 | all-reduce | flops 1 | bytes 8 | tf_op jit(solution)/shard_map/psum | solution.py:20
  2303.5 0.6 multiply_add_fusion.1
  2304.1 0.6 multiply_add_fusion
  2304.7 0.6 multiply_add_fusion.4
  (16 shorter events, 0.3 us)
Async XLA Ops:
  7.2 1.6 copy-start
  7.2 617.4 %all-reduce.9.cloned.1.call-start = ((), (), s32[]{:S(2)}) async-start(), calls=%async_computation | async-start | bytes 2097152 | tf_op jit(solution)/shard_map/psum | solution.py:81
  8.8 1.6 copy-start.3
  8.8 1.8 copy-start.1
  8.8 131.3 %copy-start.2 = (bf16[32,64]{1,0:T(8,128)(2,1)S(1)}, bf16[32,64]{1,0:T(8,128)(2,1)}, u32[]{:S(2)}) copy-start(bf16[32,64]{1,0:T(8,128)(2,1)} %param.5) | copy-start | bytes 12292
Sparse Core Ops, SparseCore 0:
  13.4 480.2 all-reduce.8
where the time goes:
time: 2310 us
  blocking collectives  2270 us (98%)
  between operations  24.6 us (1%)
    psum x2, blocking collectives, on_device(): lax.psum((part_c, own_gram_a, own_gram_b), 'wide')  834 us
    psum x4, blocking collectives, combine_dot(): return lax.psum(wide_part, 'wide') + lax.psum(narrow_part, 'narrow')  706 us
    psum x1, blocking collectives, gram_product(): cross_a, cross_b = lax.psum((local_a, local_b), 'wide')  412 us
    all_gather x1, blocking collectives, on_device(): lax.all_gather(factor_b, 'wide', axis=1, tiled=True)  129 us
    psum x2, blocking collectives, gram_product(): cross_c = lax.psum(local_c, 'narrow')  122 us
    psum x1, blocking collectives, on_device(): mttkrp_a, gram_c = lax.psum((part_a, own_gram_c), 'narrow')  66.7 us
  transfers between devices with their start and end apart: 1, of which 0 were waited for; matrix products, arithmetic and copies ran while one was open for 0% of the time, Pallas kernels for 0%

commit v1 on v0

--- a/solution.py
+++ b/solution.py
@@ -2,10 +2,14 @@
 import jax.numpy as jnp
 from jax import lax
 from jax.sharding import PartitionSpec as P
+from jax.lax import all_to_all, axis_size
 
 ITERS = 2
 damping = 1.0
 highest = lax.Precision.HIGHEST
+_render_blocks = lambda in_array, axis_id: jnp.concatenate(
+    all_to_all(jnp.stack([in_array for _ in range(axis_size(axis_id))], 0), axis_id, 0, 0), 1
+)
 
 
 def matmul(left, right):
@@ -57,7 +61,7 @@
     j_local = factor_b.shape[1]
     flattened = tensor.reshape(k_local * i_local, j_whole)
     contracted = lax.dot_general(
-        lax.all_gather(factor_b, "wide", axis=1, tiled=True),
+        _render_blocks(factor_b, "wide"),
         flattened,
         (((1,), (1,)), ((), ())),
         preferred_element_type=jnp.float32,

time: 2310 us -> 2210 us (0.957)
  blocking collectives: 2270 us -> 2150 us
    all_gather x1 -> x0, blocking collectives: 129 us -> none  [on_device(): lax.all_gather(factor_b, 'wide', axis=1, tiled=True)]
  transfers between devices with their start and end apart: 1 -> 2, of which waited for: 0 -> 0; matrix products, arithmetic and copies ran while one was open for 0% -> 0% of each run, Pallas kernels for 0% -> 0%
where the time goes in v1:
time: 2210 us
  blocking collectives  2150 us (97%)
  between operations  24.7 us (1%)
    psum x2, blocking collectives, on_device(): lax.psum((part_c, own_gram_a, own_gram_b), 'wide')  845 us
    psum x4, blocking collectives, combine_dot(): return lax.psum(wide_part, 'wide') + lax.psum(narrow_part, 'narrow')  706 us
    psum x1, blocking collectives, gram_product(): cross_a, cross_b = lax.psum((local_a, local_b), 'wide')  412 us
    psum x2, blocking collectives, gram_product(): cross_c = lax.psum(local_c, 'narrow')  121 us
    psum x1, blocking collectives, on_device(): mttkrp_a, gram_c = lax.psum((part_a, own_gram_c), 'narrow')  67 us
  transfers between devices with their start and end apart: 2, of which 0 were waited for; matrix products, arithmetic and copies ran while one was open for 0% of the time, Pallas kernels for 0%

profile of v1, /device:TPU:1, one launch (start us, length us, event | category | flops | bytes accessed | tf_op | source)
XLA Modules:
  0.0 2212.4 jit_solution(12543936142673916082)
XLA Ops:
  7.2 1.7 stack.2
  8.9 17.2 all-to-all-start
  26.2 0.7 convert_element_type.12
  26.9 0.7 convert_element_type.11
  27.5 1.6 convolution_bitcast_fusion
  29.2 0.1 fusion.48
  29.4 0.1 fusion.51
  29.5 418.9 %all-reduce.3 = (f32[32,32]{1,0:T(8,128)S(1)}, f32[32,32]{1,0:T(8,128)S(1)}) all-reduce(f32[32,32]{1,0:T(8,128)S(1)} %fusion.48, f32[32,32]{1,0:T(8,128)S(1)} %fusion.51), channel_id=1, replica_groups=mesh['wide'=64,'narrow'=8] {'wide'}, use_global_device_ids=true, to_apply=%region_0.0 | all-reduce | flops 2048 | bytes 16384 | tf_op jit(solution)/shard_map/psum | solution.py:78
  448.4 0.2 fusion.49
  448.6 0.2 copy.13
  448.8 0.2 reshape.26
  449.0 1.1 fusion.50
  450.1 0.3 fusion.14
  450.4 67.0 %all-reduce.6 = (f32[32,32]{1,0:T(8,128)S(1)}, f32[32,64]{1,0:T(8,128)S(1)}) all-reduce(f32[32,32]{1,0:T(8,128)S(1)} %fusion.49, f32[32,64]{1,0:T(8,128)S(1)} %bitcast.63), channel_id=1, replica_groups=mesh['wide'=64,'narrow'=8] {'narrow'}, use_global_device_ids=true, to_apply=%region_1.0 | all-reduce | flops 3072 | bytes 24576 | tf_op jit(solution)/shard_map/psum | solution.py:77
  517.4 0.1 convolution_subtract_fusion.1
  517.5 0.1 convolution_bitcast_fusion.4
  517.6 0.2 fusion.43
  517.8 0.8 convolution_subtract_fusion
  518.7 0.1 convolution_bitcast_fusion.6
  518.8 0.2 fusion.39
  519.0 0.3 fusion.12
  519.3 426.1 %all-reduce.2 = (f32[32,2]{0,1:T(2,128)S(1)}, f32[32,32]{1,0:T(8,128)S(1)}, f32[32,32]{1,0:T(8,128)S(1)}) all-reduce(f32[32,2]{0,1:T(2,128)S(1)} %bitcast.64, f32[32,32]{1,0:T(8,128)S(1)} %convolution_bitcast_fusion.6, f32[32,32]{1,0:T(8,128)S(1)} %convolution_bitcast_fusion.4), channel_id=1, replica_groups=mesh['wide'=64,'narrow'=8] {'wide'}, use_global_device_ids=true, to_apply=%region_8.0 | all-reduce | flops 2112 | bytes 16896 | tf_op jit(solution)/shard_map/psum | solution.py:78
  945.5 0.2 convolution_bitcast_fusion.5
  945.7 0.1 fusion.26
  945.8 0.8 multiply_reduce_fusion.7
  946.6 59.8 %all-reduce.5 = (f32[32,32]{1,0:T(8,128)S(1)}, f32[]{:T(128)}, f32[]{:T(128)}) all-reduce(f32[32,32]{1,0:T(8,128)S(1)} %convolution_bitcast_fusion.5, f32[]{:T(128)} %get-tuple-element.8, f32[]{:T(128)} %get-tuple-element.7), channel_id=1, replica_groups=mesh['wide'=64,'narrow'=8] {'narrow'}, use_global_device_ids=true, to_apply=%region_12.0 | all-reduce | flops 1026 | bytes 8208 | tf_op jit(solution)/shard_map/psum | solution.py:42
  1006.4 0.8 multiply_reduce_fusion.3
  1007.3 0.8 multiply_reduce_fusion.2
  1010.6 228.2 %all-reduce.1 = (f32[]{:T(128)}, f32[]{:T(128)}) all-reduce(f32[]{:T(128)S(6)} %add.140, f32[]{:T(128)S(6)} %add.148), channel_id=1, replica_groups=mesh['wide'=64,'narrow'=8] {'wide'}, use_global_device_ids=true, to_apply=%region_7.0 | all-reduce | flops 2 | bytes 16 | tf_op jit(solution)/shard_map/psum | solution.py:24
  1241.4 0.6 multiply_reduce_fusion.1
  1242.0 0.6 multiply_reduce_fusion
  1243.9 0.6 multiply_reduce_fusion.6
  1244.5 210.8 %psum.153 = f32[]{:T(128)} all-reduce(f32[]{:T(128)S(6)} %add.153), channel_id=1, replica_groups=mesh['wide'=64,'narrow'=8] {'wide'}, use_global_device_ids=true, to_apply=%region_21.0 | all-reduce | flops 1 | bytes 8 | tf_op jit(solution)/shard_map/psum | solution.py:24
  1455.4 38.9 %psum.154 = f32[]{:T(128)} all-reduce(f32[]{:T(128)} %multiply_reduce_fusion.6), channel_id=1, replica_groups=mesh['wide'=64,'narrow'=8] {'narrow'}, use_global_device_ids=true, to_apply=%region_23.0 | all-reduce | flops 1 | bytes 8 | tf_op jit(solution)/shard_map/psum | solution.py:24
  1495.7 0.1 fusion.52
  1495.8 0.1 convolution_bitcast_fusion.1
  1495.9 0.1 convolution_bitcast_fusion.3
  1496.1 0.2 fusion.53
  1496.2 0.2 convolution_bitcast_fusion.2
  1496.5 412.3 %all-reduce = (f32[32,32]{1,0:T(8,128)S(1)}, f32[32,32]{1,0:T(8,128)S(1)}) all-reduce(f32[32,32]{1,0:T(8,128)S(1)} %convolution_bitcast_fusion.3, f32[32,32]{1,0:T(8,128)S(1)} %convolution_bitcast_fusion.1), channel_id=1, replica_groups=mesh['wide'=64,'narrow'=8] {'wide'}, use_global_device_ids=true, to_apply=%region_24.0 | all-reduce | flops 2048 | bytes 16384 | tf_op jit(solution)/shard_map/psum | solution.py:41
  1908.9 0.8 fusion.11
  1909.7 61.5 %all-reduce.4 = (f32[32,32]{1,0:T(8,128)S(1)}, f32[]{:T(128)}) all-reduce(f32[32,32]{1,0:T(8,128)S(1)} %convolution_bitcast_fusion.2, f32[]{:T(128)} %fusion.11), channel_id=1, replica_groups=mesh['wide'=64,'narrow'=8] {'narrow'}, use_global_device_ids=true, to_apply=%region_25.0 | all-reduce | flops 1025 | bytes 8200 | tf_op jit(solution)/shard_map/psum | solution.py:42
  1971.2 0.7 fusion.9
  1972.0 0.7 fusion.10
  1974.0 228.4 %psum.158 = f32[]{:T(128)} all-reduce(f32[]{:T(128)S(6)} %add.164), channel_id=1, replica_groups=mesh['wide'=64,'narrow'=8] {'wide'}, use_global_device_ids=true, to_apply=%region_29.0 | all-reduce | flops 1 | bytes 8 | tf_op jit(solution)/shard_map/psum | solution.py:24
  2203.8 0.6 multiply_add_fusion.1
  2204.4 0.6 multiply_add_fusion
  2205.0 0.6 multiply_add_fusion.4
  (20 shorter events, 0.6 us)
Async XLA Ops:
  7.2 20.4 copy-start
  8.9 439.7 %all-to-all-start = ((bf16[64,32,128]{2,1,0:T(8,128)(2,1)}), bf16[64,32,128]{2,1,0:T(8,128)(2,1)S(1)}, u32[]{:S(2)}, u32[]{:S(2)}) async-start(bf16[64,32,128]{2,1,0:T(8,128)(2,1)} %stack.2), calls=%async_computation | async-start | bytes 1048576 | tf_op jit(solution)/shard_map/all_to_all | solution.py:11
  26.1 491.7 %all-reduce.9.cloned.1.call-start = ((), (), s32[]{:S(2)}) async-start(), calls=%async_computation.1 | async-start | bytes 2097152 | tf_op jit(solution)/shard_map/psum | solution.py:85
  27.5 1.6 copy-start.3
  27.5 1.7 copy-start.1
  27.5 1.8 copy-start.2
Sparse Core Ops, SparseCore 0:
  32.4 473.5 all-reduce.8
